TPU v7x, 32 devices: a whole 2x2x4 slice. The times are simulated.
32 devices in a mesh: dp: 4 (over y, x), rows: 8 (over z, core).
Axes of the slice: x: 2, y: 2, z: 4, core: 2. Of those that a mesh axis runs over, the one named last changes fastest.
Arguments:
- grad_out: bfloat16 [2048, 4096], P('dp', 'rows'), may hold values from -0.375 to 0.375
- activations: bfloat16 [2048, 4096], P('dp', 'rows'), may hold values from -6 to 6
- error_feedback: float32 [4, 4096, 4096], P('dp', 'rows'), may hold values from -6 to 6
- momentum: bfloat16 [4096, 4096], P('rows'), may hold values from -1.1953125 to 1.1953125
- right_factor: float32 [4096, 128], P('rows'), may hold values from -0.09375 to 0.09375
Outputs:
- new_error: float32 [4, 4096, 4096], P('dp', 'rows')
- new_momentum: bfloat16 [4096, 4096], P('rows')
- new_right: float32 [4096, 128], P('rows')
All inputs are finite; a program needn't handle non-finite values.
Results may differ from a plain program's by a relative error of at most 0.0012.
Values may be sent and summed in bfloat16 or wider, within the bound.
No kernel may reach another device: no remote copies, remote signals or barrier semaphores. Data moves between devices by JAX's collectives and lax.ppermute only.
A program may use at most 64 MiB of HBM per device.

v0:
```python
import jax
import jax.numpy as jnp
from jax import lax
from jax.sharding import PartitionSpec as P

PASSES = 2
MOMENTUM_RATE = 0.9
HIGHEST = lax.Precision.HIGHEST


def per_device(grad_out, activations, error_feedback, momentum, right_factor):
    replicas = lax.axis_size("dp")
    grad_local = lax.dot_general(
        grad_out,
        lax.all_gather(activations, "rows", axis=1, tiled=True),
        (((0,), (0,)), ((), ())),
        preferred_element_type=jnp.float32,
    )
    merged = grad_local + error_feedback[0]
    right_full = lax.all_gather(right_factor, "rows", axis=0, tiled=True)
    left_factor = None
    own_rows = None
    for pass_index in range(PASSES):
        local_term = jnp.dot(
            merged, right_full, precision=HIGHEST, preferred_element_type=jnp.float32
        )
        left_factor = lax.psum(local_term, "dp") / replicas
        gram_local = jnp.dot(
            left_factor.T, left_factor, precision=HIGHEST, preferred_element_type=jnp.float32
        )
        gram_matrix = lax.psum(gram_local, "rows")
        cholesky_lower = jnp.linalg.cholesky(gram_matrix)
        left_factor = jax.scipy.linalg.solve_triangular(cholesky_lower, left_factor.T, lower=True).T
        right_term = lax.dot_general(
            merged,
            left_factor,
            (((0,), (0,)), ((), ())),
            precision=HIGHEST,
            preferred_element_type=jnp.float32,
        )
        own_rows = lax.psum_scatter(right_term, "rows", scatter_dimension=0, tiled=True)
        own_rows = lax.psum(own_rows, "dp") / replicas
        right_full = lax.all_gather(own_rows, "rows", axis=0, tiled=True)
    approx = jnp.dot(
        left_factor, right_full.T, precision=HIGHEST, preferred_element_type=jnp.float32
    )
    new_error = (merged - approx)[None]
    new_momentum = (MOMENTUM_RATE * momentum.astype(jnp.float32) + approx).astype(jnp.bfloat16)
    return (new_error, new_momentum, own_rows)


def solution(mesh):
    return jax.shard_map(
        per_device,
        mesh=mesh,
        in_specs=(
            P("dp", "rows"),
            P("dp", "rows"),
            P("dp", "rows", None),
            P("rows", None),
            P("rows", None),
        ),
        out_specs=(P("dp", "rows", None), P("rows", None), P("rows", None)),
        check_vma=False,
    )
```

profile of v0, /device:TPU:0, one launch (start us, length us, event | category | flops | bytes accessed | tf_op | source)
XLA Modules:
  0.0 638.8 jit_solution(15261012926276648020)
XLA Ops:
  8.7 50.5 %all-gather.5.cloned.1.call-done = bf16[512,4096]{1,0:T(8,128)(2,1)} async-done(((bf16[512,512]{1,0:T(8,128)(2,1)}), bf16[512,4096]{1,0:T(8,128)(2,1)}) %all-gather.5.cloned.1.call-update) | async-done | bytes 4194320 | tf_op jit(solution)/shard_map/all_gather | solution.py:15
  59.2 10.5 %bitcast_add_fusion = f32[512,4096]{1,0:T(8,128)} fusion(f32[1,512,4096]{2,1,0:T(8,128)} %param.10, bf16[512,512]{1,0:T(8,128)(2,1)S(1)} %copy-done, bf16[512,4096]{1,0:T(8,128)(2,1)} %all-gather.5.cloned.1.call-done), kind=kOutput, calls=%fused_computation | convolution fusion | flops 2149580800 | bytes 21495808 | tf_op jit(solution)/shard_map/dot_general | solution.py:13
  69.7 19.1 %all-gather.7.cloned.1.call-done = f32[4096,128]{1,0:T(8,128)} async-done(((f32[512,128]{1,0:T(8,128)}), f32[4096,128]{1,0:T(8,128)}) %all-gather.7.cloned.1.call-update) | async-done | bytes 2097168 | tf_op jit(solution)/shard_map/all_gather | solution.py:20
  88.8 10.0 %fusion.26 = f32[512,128]{1,0:T(8,128)} fusion(f32[512,4096]{1,0:T(8,128)} %bitcast_add_fusion, f32[4096,128]{1,0:T(8,128)} %all-gather.7.cloned.1.call-done), kind=kOutput, calls=%fused_computation.40 | convolution fusion | flops 3221225472 | bytes 10747904 | tf_op jit(solution)/shard_map/dot_general | solution.py:24
  98.9 42.5 %all-reduce.7.cloned.1.call-done = f32[512,128]{1,0:T(8,128)} async-done(((f32[512,128]{1,0:T(8,128)}), f32[512,128]{1,0:T(8,128)}) %all-reduce.7.cloned.1.call-update) | async-done | bytes 262160 | tf_op jit(solution)/shard_map/psum | solution.py:27
  141.5 2.3 fusion.8
  144.1 54.8 %all-reduce.9.cloned.1.call-done = f32[128,128]{0,1:T(8,128)} async-done(((f32[128,128]{0,1:T(8,128)}), f32[128,128]{0,1:T(8,128)}) %all-reduce.9.cloned.1.call-update) | async-done | bytes 65552 | tf_op jit(solution)/shard_map/psum | solution.py:31
  198.9 0.9 copy.9
  199.9 0.9 fusion.19
  200.7 11.7 %cholesky.44 = f32[128,128]{1,0:T(8,128)S(1)} custom-call(f32[128,128]{1,0:T(8,128)S(1)} %fusion.19), custom_call_target="Cholesky" | custom-call | tf_op jit(solution)/shard_map/jit(cholesky)/cholesky | solution.py:32
  213.8 9.8 %custom-call.6 = f32[1,128,128]{1,2,0:T(8,128)S(1)} custom-call(f32[1,128,128]{2,1,0:T(8,128)S(1)} %fusion.14), custom_call_target="InvertDiagBlocksLowerTriangular" | custom-call | tf_op jit(solution)/shard_map/jit(_solve_triangular)/triangular_solve | solution.py:33
  223.6 1.4 fusion.2
  225.0 17.1 %fusion.27 = f32[4096,128]{1,0:T(8,128)} fusion(f32[512,4096]{1,0:T(8,128)} %bitcast_add_fusion, f32[128,512]{1,0:T(8,128)S(1)} %fusion.2), kind=kOutput, calls=%fused_computation.41 | convolution fusion | flops 3221225472 | bytes 10747904 | tf_op jit(solution)/shard_map/dot_general | solution.py:34
  242.1 35.2 %reduce-scatter.3.cloned.1.call-done = f32[512,128]{1,0:T(8,128)} async-done(((f32[4096,128]{1,0:T(8,128)}), f32[512,128]{1,0:T(8,128)}) %reduce-scatter.3.cloned.1.call-update) | async-done | bytes 262160 | tf_op jit(solution)/shard_map/reduce_scatter | solution.py:41
  277.4 44.3 %all-reduce.11.cloned.1.call-done = f32[512,128]{1,0:T(8,128)} async-done(((f32[512,128]{1,0:T(8,128)}), f32[512,128]{1,0:T(8,128)}) %all-reduce.11.cloned.1.call-update) | async-done | bytes 262160 | tf_op jit(solution)/shard_map/psum | solution.py:42
  321.7 1.7 broadcast_multiply_fusion.1
  323.5 29.6 %all-gather.9.cloned.1.call-done = f32[4096,128]{1,0:T(8,128)} async-done(((f32[512,128]{1,0:T(8,128)}), f32[4096,128]{1,0:T(8,128)}) %all-gather.9.cloned.1.call-update) | async-done | bytes 2097168 | tf_op jit(solution)/shard_map/all_gather | solution.py:43
  353.1 10.0 %fusion.28 = f32[512,128]{1,0:T(8,128)} fusion(f32[512,4096]{1,0:T(8,128)} %bitcast_add_fusion, f32[4096,128]{1,0:T(8,128)} %all-gather.9.cloned.1.call-done), kind=kOutput, calls=%fused_computation.42 | convolution fusion | flops 3221225472 | bytes 10747904 | tf_op jit(solution)/shard_map/dot_general | solution.py:24
  363.2 42.5 %all-reduce.13.cloned.1.call-done = f32[512,128]{1,0:T(8,128)} async-done(((f32[512,128]{1,0:T(8,128)}), f32[512,128]{1,0:T(8,128)}) %all-reduce.13.cloned.1.call-update) | async-done | bytes 262160 | tf_op jit(solution)/shard_map/psum | solution.py:27
  405.7 2.3 fusion.5
  408.3 55.1 %all-reduce.15.cloned.1.call-done = f32[128,128]{0,1:T(8,128)} async-done(((f32[128,128]{0,1:T(8,128)}), f32[128,128]{0,1:T(8,128)}) %all-reduce.15.cloned.1.call-update) | async-done | bytes 65552 | tf_op jit(solution)/shard_map/psum | solution.py:31
  463.4 0.9 copy.11
  464.3 0.9 fusion.17
  465.2 11.7 %cholesky.55 = f32[128,128]{1,0:T(8,128)S(1)} custom-call(f32[128,128]{1,0:T(8,128)S(1)} %fusion.17), custom_call_target="Cholesky" | custom-call | tf_op jit(solution)/shard_map/jit(cholesky)/cholesky | solution.py:32
  478.2 9.8 %custom-call.7 = f32[1,128,128]{1,2,0:T(8,128)S(1)} custom-call(f32[1,128,128]{2,1,0:T(8,128)S(1)} %fusion.15), custom_call_target="InvertDiagBlocksLowerTriangular" | custom-call | tf_op jit(solution)/shard_map/jit(_solve_triangular)/triangular_solve | solution.py:33
  488.0 1.4 fusion
  489.4 16.8 %fusion.29 = f32[4096,128]{1,0:T(8,128)} fusion(f32[512,4096]{1,0:T(8,128)} %bitcast_add_fusion, f32[128,512]{1,0:T(8,128)S(1)} %fusion), kind=kOutput, calls=%fused_computation.43 | convolution fusion | flops 3221225472 | bytes 10747904 | tf_op jit(solution)/shard_map/dot_general | solution.py:34
  506.2 35.2 %reduce-scatter.5.cloned.1.call-done = f32[512,128]{1,0:T(8,128)} async-done(((f32[4096,128]{1,0:T(8,128)}), f32[512,128]{1,0:T(8,128)}) %reduce-scatter.5.cloned.1.call-update) | async-done | bytes 262160 | tf_op jit(solution)/shard_map/reduce_scatter | solution.py:41
  541.5 44.5 %all-reduce.17.cloned.1.call-done = f32[512,128]{1,0:T(8,128)} async-done(((f32[512,128]{1,0:T(8,128)}), f32[512,128]{1,0:T(8,128)}) %all-reduce.17.cloned.1.call-update) | async-done | bytes 262160 | tf_op jit(solution)/shard_map/psum | solution.py:42
  586.1 1.7 broadcast_multiply_fusion
  587.8 29.5 %all-gather.11.cloned.1.call-done = f32[4096,128]{1,0:T(8,128)} async-done(((f32[512,128]{1,0:T(8,128)}), f32[4096,128]{1,0:T(8,128)}) %all-gather.11.cloned.1.call-update) | async-done | bytes 2097168 | tf_op jit(solution)/shard_map/all_gather | solution.py:43
  617.3 14.5 %add_convert_fusion = (bf16[512,4096]{1,0:T(8,128)(2,1)}, f32[1,512,4096]{2,1,0:T(8,128)}) fusion(bf16[512,4096]{1,0:T(8,128)(2,1)} %param.11, f32[512,4096]{1,0:T(8,128)} %bitcast_add_fusion, f32[128,512]{1,0:T(8,128)S(1)} %fusion, f32[4096,128]{1,0:T(8,128)} %all-gather.11.cloned.1.call-done), kind=kOutput, calls=%fused_computation.1 | convolution fusion | flops 3231711232 | bytes 27525120 | tf_op jit(solution)/shard_map/dot_general | solution.py:44
  (32 shorter events, 5.2 us)
Async XLA Ops:
  7.2 52.1 %copy-start = (bf16[512,512]{1,0:T(8,128)(2,1)S(1)}, bf16[512,512]{1,0:T(8,128)(2,1)}, u32[]{:S(2)}) copy-start(bf16[512,512]{1,0:T(8,128)(2,1)} %param.8) | copy-start | bytes 1572868
  7.2 52.0 %all-gather.5.cloned.1.call-start = ((), (), s32[]{:S(2)}) async-start(), calls=%async_computation.2 | async-start | bytes 4718592 | tf_op jit(solution)/shard_map/all_gather | solution.py:15
  7.9 80.9 %all-gather.7.cloned.1.call-start = ((), (), s32[]{:S(2)}) async-start(), calls=%async_computation.3 | async-start | bytes 2359296 | tf_op jit(solution)/shard_map/all_gather | solution.py:20
  8.7 132.8 %all-reduce.7.cloned.1.call-start = ((), (), s32[]{:S(2)}) async-start(), calls=%async_computation.4 | async-start | bytes 524288 | tf_op jit(solution)/shard_map/psum | solution.py:27
  98.9 100.1 %all-reduce.9.cloned.1.call-start = ((), (), s32[]{:S(2)}) async-start(), calls=%async_computation.5 | async-start | bytes 131072 | tf_op jit(solution)/shard_map/psum | solution.py:31
  143.7 133.6 %reduce-scatter.3.cloned.1.call-start = ((), (), s32[]{:S(2)}) async-start(), calls=%async_computation.6 | async-start | bytes 2359296 | tf_op jit(solution)/shard_map/reduce_scatter | solution.py:41
  242.1 79.7 %all-reduce.11.cloned.1.call-start = ((), (), s32[]{:S(2)}) async-start(), calls=%async_computation.7 | async-start | bytes 524288 | tf_op jit(solution)/shard_map/psum | solution.py:42
  277.3 75.7 %all-gather.9.cloned.1.call-start = ((), (), s32[]{:S(2)}) async-start(), calls=%async_computation.8 | async-start | bytes 2359296 | tf_op jit(solution)/shard_map/all_gather | solution.py:43
  323.4 82.3 %all-reduce.13.cloned.1.call-start = ((), (), s32[]{:S(2)}) async-start(), calls=%async_computation.9 | async-start | bytes 524288 | tf_op jit(solution)/shard_map/psum | solution.py:27
  363.2 100.2 %all-reduce.15.cloned.1.call-start = ((), (), s32[]{:S(2)}) async-start(), calls=%async_computation.10 | async-start | bytes 131072 | tf_op jit(solution)/shard_map/psum | solution.py:31
  408.0 133.4 %reduce-scatter.5.cloned.1.call-start = ((), (), s32[]{:S(2)}) async-start(), calls=%async_computation.11 | async-start | bytes 2359296 | tf_op jit(solution)/shard_map/reduce_scatter | solution.py:41
  506.2 79.9 %all-reduce.17.cloned.1.call-start = ((), (), s32[]{:S(2)}) async-start(), calls=%async_computation.12 | async-start | bytes 524288 | tf_op jit(solution)/shard_map/psum | solution.py:42
  541.5 75.8 %all-gather.11.cloned.1.call-start = ((), (), s32[]{:S(2)}) async-start(), calls=%async_computation.13 | async-start | bytes 2359296 | tf_op jit(solution)/shard_map/all_gather | solution.py:43
Sparse Core Ops, SparseCore 0:
  9.6 49.5 all-gather.4
  60.8 27.9 all-gather.6
  99.0 42.4 all-reduce.6
  144.2 54.6 all-reduce.8
  242.2 35.0 reduce-scatter.2
  280.1 41.5 all-reduce.10
  323.9 29.1 all-gather.8
  363.3 42.4 all-reduce.12
  408.6 54.6 all-reduce.14
  506.3 35.1 reduce-scatter.4
  544.4 41.6 all-reduce.16
  588.1 29.1 all-gather.10
where the time goes:
time: 644 us; the launch traced here: 639 us
  waiting for transfers between devices  485 us (75%)
  matrix products  86.1 us (13%)
  other arithmetic  50.8 us (8%)
  between operations  14.5 us (2%)
    psum x2, waiting for transfers between devices, per_device(): gram_matrix = lax.psum(gram_local, 'rows')  110 us
    psum x2, waiting for transfers between devices, per_device(): own_rows = lax.psum(own_rows, 'dp') / replicas  88.9 us
    psum x2, waiting for transfers between devices, per_device(): left_factor = lax.psum(local_term, 'dp') / replicas  85.1 us
    reduce_scatter x2, waiting for transfers between devices, per_device(): lax.psum_scatter(right_term, 'rows', scatter_dimension=0, tiled=True)  70.4 us
    all_gather x2, waiting for transfers between devices, per_device(): right_full = lax.all_gather(own_rows, 'rows', axis=0, tiled=True)  59.1 us
    all_gather x1, waiting for transfers between devices, per_device(): lax.all_gather(activations, 'rows', axis=1, tiled=True)  50.5 us
    dot_general x2, matrix products, per_device(): lax.dot_general(merged, left_factor, (((0,), (0,)), ((), ())), precision=...  33.8 us
    another operation x6, other arithmetic, per_device(): cholesky_lower = jnp.linalg.cholesky(gram_matrix)  24.8 us
  transfers between devices with their start and end apart: 12, of which 12 were waited for; matrix products, arithmetic and copies ran while one was open for 2% of the time, Pallas kernels for 0%

commit v1 on v0

--- a/solution.py
+++ b/solution.py
@@ -28,7 +28,11 @@
         gram_local = jnp.dot(
             left_factor.T, left_factor, precision=HIGHEST, preferred_element_type=jnp.float32
         )
-        gram_matrix = lax.psum(gram_local, "rows")
+        gram_matrix = gram_local
+        for hop in (1, 2, 4):
+            gram_matrix = gram_matrix + lax.ppermute(
+                gram_matrix, "rows", [(dev, dev ^ hop) for dev in range(8)]
+            )
         cholesky_lower = jnp.linalg.cholesky(gram_matrix)
         left_factor = jax.scipy.linalg.solve_triangular(cholesky_lower, left_factor.T, lower=True).T
         right_term = lax.dot_general(

time: 644 us -> 554 us (0.86)
  waiting for transfers between devices: 485 us -> 391 us
  starting transfers between devices: 0.95 us -> 9.05 us
    psum x2 -> x0, waiting for transfers between devices: 110 us -> none  [per_device(): gram_matrix = lax.psum(gram_local, 'rows')]
    ppermute x0 -> x6, waiting for transfers between devices: none -> 13.6 us  [per_device(): lax.ppermute(gram_matrix, 'rows', [(dev, dev ^ hop) for dev in range(8)])]
    ppermute x0 -> x6, starting transfers between devices: none -> 8.19 us  [per_device(): lax.ppermute(gram_matrix, 'rows', [(dev, dev ^ hop) for dev in range(8)])]
  transfers between devices with their start and end apart: 12 -> 16, of which waited for: 12 -> 16; matrix products, arithmetic and copies ran while one was open for 2% -> 2% of each run, Pallas kernels for 0% -> 0%
where the time goes in v1:
time: 554 us; the launch traced here: 549 us
  waiting for transfers between devices  391 us (71%)
  matrix products  84.8 us (15%)
  other arithmetic  49.1 us (9%)
  between operations  14.5 us (3%)
  starting transfers between devices  9.05 us (2%)
    psum x2, waiting for transfers between devices, per_device(): own_rows = lax.psum(own_rows, 'dp') / replicas  89 us
    psum x2, waiting for transfers between devices, per_device(): left_factor = lax.psum(local_term, 'dp') / replicas  84.6 us
    reduce_scatter x2, waiting for transfers between devices, per_device(): lax.psum_scatter(right_term, 'rows', scatter_dimension=0, tiled=True)  73.6 us
    all_gather x2, waiting for transfers between devices, per_device(): right_full = lax.all_gather(own_rows, 'rows', axis=0, tiled=True)  59 us
    all_gather x1, waiting for transfers between devices, per_device(): lax.all_gather(activations, 'rows', axis=1, tiled=True)  50.5 us
    dot_general x2, matrix products, per_device(): lax.dot_general(merged, left_factor, (((0,), (0,)), ((), ())), precision=...  33.8 us
    another operation x6, other arithmetic, per_device(): cholesky_lower = jnp.linalg.cholesky(gram_matrix)  24.8 us
    another operation x4, other arithmetic, per_device(): jax.scipy.linalg.solve_triangular(cholesky_lower, left_factor.T, lower=True)  20.9 us
  transfers between devices with their start and end apart: 16, of which 16 were waited for; matrix products, arithmetic and copies ran while one was open for 2% of the time, Pallas kernels for 0%

profile of v1, /device:TPU:0, one launch (start us, length us, event | category | flops | bytes accessed | tf_op | source)
XLA Modules:
  0.0 548.7 jit_solution(17888350181133115206)
XLA Ops:
  8.7 50.5 %all-gather.5.cloned.1.call-done = bf16[512,4096]{1,0:T(8,128)(2,1)} async-done(((bf16[512,512]{1,0:T(8,128)(2,1)}), bf16[512,4096]{1,0:T(8,128)(2,1)}) %all-gather.5.cloned.1.call-update) | async-done | bytes 4194320 | tf_op jit(solution)/shard_map/all_gather | solution.py:15
  59.2 10.5 %bitcast_add_fusion = f32[512,4096]{1,0:T(8,128)} fusion(f32[1,512,4096]{2,1,0:T(8,128)} %param.10, bf16[512,512]{1,0:T(8,128)(2,1)S(1)} %copy-done, bf16[512,4096]{1,0:T(8,128)(2,1)} %all-gather.5.cloned.1.call-done), kind=kOutput, calls=%fused_computation | convolution fusion | flops 2149580800 | bytes 21495808 | tf_op jit(solution)/shard_map/dot_general | solution.py:13
  69.7 19.1 %all-gather.7.cloned.1.call-done = f32[4096,128]{1,0:T(8,128)} async-done(((f32[512,128]{1,0:T(8,128)}), f32[4096,128]{1,0:T(8,128)}) %all-gather.7.cloned.1.call-update) | async-done | bytes 2097168 | tf_op jit(solution)/shard_map/all_gather | solution.py:20
  88.8 10.0 %fusion.26 = f32[512,128]{1,0:T(8,128)} fusion(f32[512,4096]{1,0:T(8,128)} %bitcast_add_fusion, f32[4096,128]{1,0:T(8,128)} %all-gather.7.cloned.1.call-done), kind=kOutput, calls=%fused_computation.40 | convolution fusion | flops 3221225472 | bytes 10747904 | tf_op jit(solution)/shard_map/dot_general | solution.py:24
  99.2 42.3 %all-reduce.5.cloned.1.call-done = f32[512,128]{1,0:T(8,128)} async-done(((f32[512,128]{1,0:T(8,128)}), f32[512,128]{1,0:T(8,128)}) %all-reduce.5.cloned.1.call-update) | async-done | bytes 262160 | tf_op jit(solution)/shard_map/psum | solution.py:27
  141.5 1.6 fusion.8
  144.4 1.6 collective-permute-start.1
  146.0 2.8 collective-permute-done.1
  148.8 2.5 collective-permute-start.2
  151.2 2.8 collective-permute-done.2
  154.1 11.7 %cholesky.44 = f32[128,128]{1,0:T(8,128)S(1)} custom-call(f32[128,128]{1,0:T(8,128)S(1)} %fusion.19), custom_call_target="Cholesky" | custom-call | tf_op jit(solution)/shard_map/jit(cholesky)/cholesky | solution.py:36
  167.2 9.8 %custom-call.6 = f32[1,128,128]{1,2,0:T(8,128)S(1)} custom-call(f32[1,128,128]{2,1,0:T(8,128)S(1)} %fusion.14), custom_call_target="InvertDiagBlocksLowerTriangular" | custom-call | tf_op jit(solution)/shard_map/jit(_solve_triangular)/triangular_solve | solution.py:37
  178.4 17.1 %fusion.27 = f32[4096,128]{1,0:T(8,128)} fusion(f32[512,4096]{1,0:T(8,128)} %bitcast_add_fusion, f32[128,512]{1,0:T(8,128)S(1)} %fusion.2), kind=kOutput, calls=%fused_computation.41 | convolution fusion | flops 3221225472 | bytes 10747904 | tf_op jit(solution)/shard_map/dot_general | solution.py:38
  195.5 36.8 %reduce-scatter.3.cloned.1.call-done = f32[512,128]{1,0:T(8,128)} async-done(((f32[4096,128]{1,0:T(8,128)}), f32[512,128]{1,0:T(8,128)}) %reduce-scatter.3.cloned.1.call-update) | async-done | bytes 262160 | tf_op jit(solution)/shard_map/reduce_scatter | solution.py:45
  232.4 44.4 %all-reduce.7.cloned.1.call-done = f32[512,128]{1,0:T(8,128)} async-done(((f32[512,128]{1,0:T(8,128)}), f32[512,128]{1,0:T(8,128)}) %all-reduce.7.cloned.1.call-update) | async-done | bytes 262160 | tf_op jit(solution)/shard_map/psum | solution.py:46
  276.8 1.7 broadcast_multiply_fusion.1
  278.5 29.5 %all-gather.9.cloned.1.call-done = f32[4096,128]{1,0:T(8,128)} async-done(((f32[512,128]{1,0:T(8,128)}), f32[4096,128]{1,0:T(8,128)}) %all-gather.9.cloned.1.call-update) | async-done | bytes 2097168 | tf_op jit(solution)/shard_map/all_gather | solution.py:47
  308.0 10.0 %fusion.28 = f32[512,128]{1,0:T(8,128)} fusion(f32[512,4096]{1,0:T(8,128)} %bitcast_add_fusion, f32[4096,128]{1,0:T(8,128)} %all-gather.9.cloned.1.call-done), kind=kOutput, calls=%fused_computation.42 | convolution fusion | flops 3221225472 | bytes 10747904 | tf_op jit(solution)/shard_map/dot_general | solution.py:24
  318.3 42.4 %all-reduce.9.cloned.1.call-done = f32[512,128]{1,0:T(8,128)} async-done(((f32[512,128]{1,0:T(8,128)}), f32[512,128]{1,0:T(8,128)}) %all-reduce.9.cloned.1.call-update) | async-done | bytes 262160 | tf_op jit(solution)/shard_map/psum | solution.py:27
  360.6 1.6 fusion.5
  363.6 1.6 collective-permute-start.4
  365.2 2.8 collective-permute-done.4
  367.9 2.5 collective-permute-start.5
  370.4 2.8 collective-permute-done.5
  373.3 11.7 %cholesky.55 = f32[128,128]{1,0:T(8,128)S(1)} custom-call(f32[128,128]{1,0:T(8,128)S(1)} %fusion.17), custom_call_target="Cholesky" | custom-call | tf_op jit(solution)/shard_map/jit(cholesky)/cholesky | solution.py:36
  386.4 9.8 %custom-call.7 = f32[1,128,128]{1,2,0:T(8,128)S(1)} custom-call(f32[1,128,128]{2,1,0:T(8,128)S(1)} %fusion.15), custom_call_target="InvertDiagBlocksLowerTriangular" | custom-call | tf_op jit(solution)/shard_map/jit(_solve_triangular)/triangular_solve | solution.py:37
  397.6 16.8 %fusion.29 = f32[4096,128]{1,0:T(8,128)} fusion(f32[512,4096]{1,0:T(8,128)} %bitcast_add_fusion, f32[128,512]{1,0:T(8,128)S(1)} %fusion), kind=kOutput, calls=%fused_computation.43 | convolution fusion | flops 3221225472 | bytes 10747904 | tf_op jit(solution)/shard_map/dot_general | solution.py:38
  414.4 36.8 %reduce-scatter.5.cloned.1.call-done = f32[512,128]{1,0:T(8,128)} async-done(((f32[4096,128]{1,0:T(8,128)}), f32[512,128]{1,0:T(8,128)}) %reduce-scatter.5.cloned.1.call-update) | async-done | bytes 262160 | tf_op jit(solution)/shard_map/reduce_scatter | solution.py:45
  451.3 44.7 %all-reduce.11.cloned.1.call-done = f32[512,128]{1,0:T(8,128)} async-done(((f32[512,128]{1,0:T(8,128)}), f32[512,128]{1,0:T(8,128)}) %all-reduce.11.cloned.1.call-update) | async-done | bytes 262160 | tf_op jit(solution)/shard_map/psum | solution.py:46
  496.0 1.7 broadcast_multiply_fusion
  497.6 29.5 %all-gather.11.cloned.1.call-done = f32[4096,128]{1,0:T(8,128)} async-done(((f32[512,128]{1,0:T(8,128)}), f32[4096,128]{1,0:T(8,128)}) %all-gather.11.cloned.1.call-update) | async-done | bytes 2097168 | tf_op jit(solution)/shard_map/all_gather | solution.py:47
  527.2 14.5 %add_convert_fusion = (bf16[512,4096]{1,0:T(8,128)(2,1)}, f32[1,512,4096]{2,1,0:T(8,128)}) fusion(bf16[512,4096]{1,0:T(8,128)(2,1)} %param.11, f32[512,4096]{1,0:T(8,128)} %bitcast_add_fusion, f32[128,512]{1,0:T(8,128)S(1)} %fusion, f32[4096,128]{1,0:T(8,128)} %all-gather.11.cloned.1.call-done), kind=kOutput, calls=%fused_computation.1 | convolution fusion | flops 3231711232 | bytes 27525120 | tf_op jit(solution)/shard_map/dot_general | solution.py:48
  (44 shorter events, 10.7 us)
Async XLA Ops:
  7.2 52.1 %copy-start = (bf16[512,512]{1,0:T(8,128)(2,1)S(1)}, bf16[512,512]{1,0:T(8,128)(2,1)}, u32[]{:S(2)}) copy-start(bf16[512,512]{1,0:T(8,128)(2,1)} %param.8) | copy-start | bytes 1572868
  7.2 52.0 %all-gather.5.cloned.1.call-start = ((), (), s32[]{:S(2)}) async-start(), calls=%async_computation.2 | async-start | bytes 4718592 | tf_op jit(solution)/shard_map/all_gather | solution.py:15
  7.9 80.9 %all-gather.7.cloned.1.call-start = ((), (), s32[]{:S(2)}) async-start(), calls=%async_computation.3 | async-start | bytes 2359296 | tf_op jit(solution)/shard_map/all_gather | solution.py:20
  8.7 132.8 %all-reduce.5.cloned.1.call-start = ((), (), s32[]{:S(2)}) async-start(), calls=%async_computation.4 | async-start | bytes 524288 | tf_op jit(solution)/shard_map/psum | solution.py:27
  98.9 133.5 %reduce-scatter.3.cloned.1.call-start = ((), (), s32[]{:S(2)}) async-start(), calls=%async_computation.5 | async-start | bytes 2359296 | tf_op jit(solution)/shard_map/reduce_scatter | solution.py:45
  143.1 1.3 collective-permute-start
  144.4 4.3 collective-permute-start.1
  148.8 5.2 collective-permute-start.2
  195.5 81.3 %all-reduce.7.cloned.1.call-start = ((), (), s32[]{:S(2)}) async-start(), calls=%async_computation.6 | async-start | bytes 524288 | tf_op jit(solution)/shard_map/psum | solution.py:46
  232.4 75.6 %all-gather.9.cloned.1.call-start = ((), (), s32[]{:S(2)}) async-start(), calls=%async_computation.7 | async-start | bytes 2359296 | tf_op jit(solution)/shard_map/all_gather | solution.py:47
  278.5 82.2 %all-reduce.9.cloned.1.call-start = ((), (), s32[]{:S(2)}) async-start(), calls=%async_computation.8 | async-start | bytes 524288 | tf_op jit(solution)/shard_map/psum | solution.py:27
  318.0 133.2 %reduce-scatter.5.cloned.1.call-start = ((), (), s32[]{:S(2)}) async-start(), calls=%async_computation.9 | async-start | bytes 2359296 | tf_op jit(solution)/shard_map/reduce_scatter | solution.py:45
  362.3 1.3 collective-permute-start.3
  363.6 4.3 collective-permute-start.4
  367.9 5.2 collective-permute-start.5
  414.3 81.6 %all-reduce.11.cloned.1.call-start = ((), (), s32[]{:S(2)}) async-start(), calls=%async_computation.10 | async-start | bytes 524288 | tf_op jit(solution)/shard_map/psum | solution.py:46
  451.2 75.9 %all-gather.11.cloned.1.call-start = ((), (), s32[]{:S(2)}) async-start(), calls=%async_computation.11 | async-start | bytes 2359296 | tf_op jit(solution)/shard_map/all_gather | solution.py:47
Sparse Core Ops, SparseCore 0:
  9.6 49.5 all-gather.4
  60.8 27.9 all-gather.6
  99.0 42.4 all-reduce.4
  195.6 36.6 reduce-scatter.2
  235.1 41.6 all-reduce.6
  278.8 29.1 all-gather.8
  318.2 42.4 all-reduce.8
  414.5 36.7 reduce-scatter.4
  454.1 41.7 all-reduce.10
  498.0 29.1 all-gather.10
